TPU v7x, 32 devices: a whole 2x2x4 slice. The times are simulated.
32 devices in a mesh: grp: 2 (over x), mod: 16 (over z, y, core).
Axes of the slice: x: 2, y: 2, z: 4, core: 2. Of those that a mesh axis runs over, the one named last changes fastest.
Arguments:
- inputs_proj: bfloat16 [128, 16, 1536], P(('grp', 'mod')), parts along dimension 0, may hold values from -2.5 to 2.5
- outputs_proj: bfloat16 [128, 16, 1280], P(('grp', 'mod')), parts along dimension 0, may hold values from -2.5 to 2.5
- lengths: int32 [128], P(('grp', 'mod')), parts along dimension 0, may hold values from 16 to 32, as said below
- owner: int32 [16], replicated, may hold values from 0 to 15, each once
- fisher_inv: bfloat16 [16, 1920, 1920], P('mod'), may hold values from -25 to 25, as said below
- query_grads: bfloat16 [16, 512, 1920], P('mod'), may hold values from -0.03125 to 0.03125
Outputs:
- scores: float32 [128, 512], P(('grp', 'mod')), parts along dimension 0
There are 2 independent parts, one for each index of `grp`. A program takes and returns all parts, laid end to end along the dimension named above; an argument that names none is the same for every part. Nothing has to cross between parts.
Inputs may be any that keep to these rules, and one draw needn't show every extreme that they name: `fisher_inv`: each matrix is symmetric. `lengths`: some example of each group has all 32 slots live.
All inputs are finite; a program needn't handle non-finite values.
Results may differ from a plain program's by a relative error of at most 0.0041.
Values may be sent and summed in bfloat16 or wider, within the bound.
No kernel may reach another device: no remote copies, remote signals or barrier semaphores. Data moves between devices by JAX's collectives and lax.ppermute only.
A program may use at most 128 MiB of HBM per device.

v0:
```python
import jax
import jax.numpy as jnp
from jax import lax
from jax.sharding import PartitionSpec as P

OUT_RANK = 40
IN_RANK = 48
SEQ_LEN = 32


def masked(source, lengths, features):
    count_rows = source.shape[0]
    count_modules = source.shape[1]
    live = (lax.broadcasted_iota(jnp.int32, (count_rows, SEQ_LEN), 1) < lengths[:, None]).astype(
        source.dtype
    )
    return source.reshape(count_rows, count_modules, features, SEQ_LEN) * live[:, None, None, :]


def outer_grads(side_out, side_in):
    formed = jnp.einsum("emol,emil->emoi", side_out, side_in, preferred_element_type=jnp.float32)
    return formed.astype(jnp.bfloat16)


def local(inputs_proj, outputs_proj, lengths, owner, fisher_inv, query_grads):
    count_modules = owner.shape[0]
    local_rows = inputs_proj.shape[0]
    local_in = masked(inputs_proj, lengths, IN_RANK)
    local_out = masked(outputs_proj, lengths, OUT_RANK)
    inverse = (
        jnp.zeros((count_modules,), jnp.int32)
        .at[owner]
        .set(jnp.arange(count_modules, dtype=jnp.int32))
    )
    precond = jnp.dot(query_grads[0], fisher_inv[0], preferred_element_type=jnp.float32).astype(
        jnp.bfloat16
    )
    formed = outer_grads(local_out, local_in).reshape(local_rows, count_modules, OUT_RANK * IN_RANK)
    routed = jnp.take(formed, inverse, axis=1)
    received = lax.all_to_all(routed, "mod", split_axis=1, concat_axis=0, tiled=True)
    example_grads = received.reshape(received.shape[0], OUT_RANK * IN_RANK)
    return lax.psum_scatter(
        lax.dot_general(
            example_grads, precond, (((1,), (1,)), ((), ())), preferred_element_type=jnp.float32
        ),
        "mod",
        scatter_dimension=0,
        tiled=True,
    )


def solution(mesh):
    return jax.shard_map(
        local,
        mesh=mesh,
        in_specs=(
            P(("grp", "mod"), None, None),
            P(("grp", "mod"), None, None),
            P(("grp", "mod")),
            P(),
            P("mod", None, None),
            P("mod", None, None),
        ),
        out_specs=P(("grp", "mod"), None),
        check_vma=False,
    )
```

profile of v0, /device:TPU:0, one launch (start us, length us, event | category | flops | bytes accessed | tf_op | source)
XLA Modules:
  0.0 136.1 jit_solution(4244372473379199005)
XLA Ops:
  6.5 0.0 copy-start
  6.5 0.0 all-reduce.3.cloned.1.call-start
  6.5 0.8 compare_select_fusion.1
  7.3 0.6 scatter_custom_fusion
  8.0 1.5 %reshape.35 = bf16[4,16,48,32]{3,2,1,0:T(8,128)(2,1)S(1)} reshape(bf16[4,16,1536]{2,1,0:T(8,128)(2,1)} %param.6) | data formatting | bytes 393216 | tf_op jit(solution)/shard_map/reshape | solution.py:17
  9.5 2.3 %reshape.34 = bf16[4,16,40,32]{3,2,1,0:T(8,128)(2,1)} reshape(bf16[4,16,1280]{2,1,0:T(8,128)(2,1)} %param.7) | data formatting | bytes 327680 | tf_op jit(solution)/shard_map/reshape | solution.py:17
  11.7 0.7 fusion.15
  12.4 1.6 %convolution_convert_fusion = bf16[4,16,40,48]{3,2,1,0:T(8,128)(2,1)S(1)} fusion(bf16[4,16,48,32]{3,2,1,0:T(8,128)(2,1)S(1)} %reshape.35, bf16[4,16,40,32]{3,2,1,0:T(8,128)(2,1)} %reshape.34, bf16[4,32]{1,0:T(4,128)(2,1)S(1)} %fusion.15), kind=kOutput, calls=%fused_computation.6 | convolution fusion | flops 8167424 | bytes 606464 | tf_op jit(solution)/shard_map/emol,emil->emoi/dot_general | solution.py:21
  14.1 0.4 reshape.36
  14.5 0.1 copy.14
  14.6 0.8 gather_fusion
  15.4 0.2 select_bitcast_fusion
  15.6 17.0 %all_to_all.15 = bf16[4,16,1920]{2,0,1:T(4,128)(2,1)S(1)} all-to-all(bf16[4,16,1920]{2,0,1:T(4,128)(2,1)S(1)} %select_bitcast_fusion), channel_id=1, replica_groups=mesh['grp'=2,'mod'=16] {'mod'}, dimensions={1} | all-to-all | bytes 491520 | tf_op jit(solution)/shard_map/all_to_all | solution.py:40
  32.6 0.1 reshape.37
  32.6 0.0 copy-done
  32.6 0.0 copy-start.1
  32.7 8.7 %fusion.8 = f32[64,512]{1,0:T(8,128)} fusion(bf16[64,1920]{1,0:T(8,128)(2,1)S(1)} %reshape.37, bf16[1,1920,1920]{2,1,0:T(8,128)(2,1)} %param.10, bf16[1,512,1920]{2,1,0:T(8,128)(2,1)S(1)} %copy-done), kind=kOutput, calls=%fused_computation.7 | convolution fusion | flops 3901685760 | bytes 9715712 | tf_op jit(solution)/shard_map/dot_general | solution.py:43
  41.4 0.0 all-reduce.3.cloned.1.call-update
  41.4 0.0 copy-done.1
  41.4 0.6 dynamic-slice
  42.6 85.3 %all-reduce.3.cloned.1.call-done = f32[64,512]{1,0:T(8,128)} async-done(((f32[64,512]{1,0:T(8,128)}), f32[64,512]{1,0:T(8,128)}) %all-reduce.3.cloned.1.call-update) | async-done | bytes 131088
  127.9 1.3 constant_dynamic-slice_fusion
  (4 shorter events, 0.0 us)
Async XLA Ops:
  6.5 26.1 %copy-start = (bf16[1,512,1920]{2,1,0:T(8,128)(2,1)S(1)}, bf16[1,512,1920]{2,1,0:T(8,128)(2,1)}, u32[]{:S(2)}) copy-start(bf16[1,512,1920]{2,1,0:T(8,128)(2,1)} %param.11) | copy-start | bytes 5898244
  6.5 121.4 %all-reduce.3.cloned.1.call-start = ((), (), s32[]{:S(2)}) async-start(), calls=%async_computation.1 | async-start | bytes 262144
  32.6 8.8 %copy-start.1 = (u32[32]{0:T(128)S(1)}, u32[32]{0:T(128)}, u32[]{:S(2)}) copy-start(u32[32]{0:T(128)} %constant.25) | copy-start | bytes 388
Sparse Core Ops, SparseCore 0:
  41.5 86.3 all-reduce.2
where the time goes:
time: 137 us; the launch traced here: 136 us
  waiting for transfers between devices  85.3 us (62%)
  blocking collectives  17 us (12%)
  between operations  14.1 us (10%)
  matrix products  10.4 us (8%)
  local copies, waits for them, and re-layouts  7.6 us (6%)
  other arithmetic  1.73 us (1%)
    unnamed x2, waiting for transfers between devices  85.3 us
    all_to_all x1, blocking collectives, local(): lax.all_to_all(routed, 'mod', split_axis=1, concat_axis=0, tiled=True)  17 us
    dot_general x1, matrix products, local(): lax.dot_general(example_grads, precond, (((1,), (1,)), ((), ())), preferr...  8.72 us
    reshape x2, local copies, waits for them, and re-layouts, masked(): source.reshape(count_rows, count_modules, features, SEQ_LEN)  3.71 us
  transfers between devices with their start and end apart: 1, of which 1 were waited for; matrix products, arithmetic and copies ran while one was open for 0% of the time, Pallas kernels for 0%

commit v1 on v0

--- a/solution.py
+++ b/solution.py
@@ -39,14 +39,17 @@
     routed = jnp.take(formed, inverse, axis=1)
     received = lax.all_to_all(routed, "mod", split_axis=1, concat_axis=0, tiled=True)
     example_grads = received.reshape(received.shape[0], OUT_RANK * IN_RANK)
-    return lax.psum_scatter(
-        lax.dot_general(
-            example_grads, precond, (((1,), (1,)), ((), ())), preferred_element_type=jnp.float32
-        ),
+    partial = lax.dot_general(
+        example_grads, precond, (((1,), (1,)), ((), ())), preferred_element_type=jnp.float32
+    )
+    spread = lax.all_to_all(
+        partial.reshape(count_modules, local_rows, partial.shape[1]),
         "mod",
-        scatter_dimension=0,
+        split_axis=0,
+        concat_axis=0,
         tiled=True,
     )
+    return jnp.sum(spread, axis=0)
 
 
 def solution(mesh):

time: 137 us -> 45.7 us (0.33)
  waiting for transfers between devices: 85.3 us -> 0 us
  between operations: 14.1 us -> 0.08 us
  blocking collectives: 17 us -> 27.5 us
  local copies, waits for them, and re-layouts: 7.6 us -> 5.7 us
    unnamed x2 -> x0, waiting for transfers between devices: 85.3 us -> none
    all_to_all x0 -> x1, blocking collectives: none -> 10.5 us  [local(): lax.all_to_all(partial.reshape(count_modules, local_rows, partial.shape[1...]
    unnamed x6 -> x2, local copies, waits for them, and re-layouts: 1.92 us -> 0.01 us
  transfers between devices with their start and end apart: 1 -> 0, of which waited for: 1 -> 0; matrix products, arithmetic and copies ran while one was open for 0% -> 0% of each run, Pallas kernels for 0% -> 0%
where the time goes in v1:
time: 45.7 us; the launch traced here: 45.3 us
  blocking collectives  27.5 us (60%)
  matrix products  9.71 us (21%)
  local copies, waits for them, and re-layouts  5.7 us (12%)
  other arithmetic  2.36 us (5%)
    all_to_all x1, blocking collectives, local(): lax.all_to_all(routed, 'mod', split_axis=1, concat_axis=0, tiled=True)  17 us
    all_to_all x1, blocking collectives, local(): lax.all_to_all(partial.reshape(count_modules, local_rows, partial.shape[1...  10.5 us
    dot_general x1, matrix products, local(): lax.dot_general(example_grads, precond, (((1,), (1,)), ((), ())), preferr...  8.06 us
    reshape x2, local copies, waits for them, and re-layouts, masked(): source.reshape(count_rows, count_modules, features, SEQ_LEN)  3.7 us
    dot_general x1, matrix products, outer_grads(): jnp.einsum('emol,emil->emoi', side_out, side_in, preferred_element_type=j...  1.64 us

profile of v1, /device:TPU:0, one launch (start us, length us, event | category | flops | bytes accessed | tf_op | source)
XLA Modules:
  0.0 45.3 jit_solution(2968081646143792824)
XLA Ops:
  0.0 0.0 copy-start
  0.0 0.8 %compare_select_fusion.1 = s32[16]{0:T(128)S(1)} fusion(s32[16]{0:T(128)} %param.9), kind=kLoop, calls=%fused_computation.18 | loop fusion | flops 48 | bytes 128 | tf_op jit(solution)/shard_map/select_n | solution.py:33
  0.8 0.6 %scatter_custom_fusion = s32[16]{0:T(128)S(1)} fusion(s32[16]{0:T(128)S(1)} %compare_select_fusion.1, s32[16]{0:T(128)S(1)} %iota.12, s32[]{:T(128)} %constant.6.clone.1), kind=kCustom, calls=%fused_computation.22 | custom fusion | bytes 68 | tf_op jit(solution)/shard_map/scatter | solution.py:33
  1.5 1.5 %reshape.36 = bf16[4,16,48,32]{3,2,1,0:T(8,128)(2,1)S(1)} reshape(bf16[4,16,1536]{2,1,0:T(8,128)(2,1)} %param.6) | data formatting | bytes 393216 | tf_op jit(solution)/shard_map/reshape | solution.py:17
  2.9 2.2 %reshape.35 = bf16[4,16,40,32]{3,2,1,0:T(8,128)(2,1)} reshape(bf16[4,16,1280]{2,1,0:T(8,128)(2,1)} %param.7) | data formatting | bytes 327680 | tf_op jit(solution)/shard_map/reshape | solution.py:17
  5.2 0.7 %fusion.20 = bf16[4,32]{1,0:T(4,128)(2,1)S(1)} fusion(s32[4]{0:T(128)} %param.8), kind=kLoop, calls=%fused_computation.20 | loop fusion | flops 256 | bytes 272 | tf_op jit(solution)/shard_map/convert_element_type | solution.py:14
  5.9 1.6 %convolution_convert_fusion = bf16[4,16,40,48]{3,2,1,0:T(8,128)(2,1)S(1)} fusion(bf16[4,16,48,32]{3,2,1,0:T(8,128)(2,1)S(1)} %reshape.36, bf16[4,16,40,32]{3,2,1,0:T(8,128)(2,1)} %reshape.35, bf16[4,32]{1,0:T(4,128)(2,1)S(1)} %fusion.20), kind=kOutput, calls=%fused_computation.7 | convolution fusion | flops 8167424 | bytes 606464 | tf_op jit(solution)/shard_map/emol,emil->emoi/dot_general | solution.py:21
  7.5 0.4 reshape.37
  8.0 0.1 copy.15
  8.1 0.8 %gather_fusion = bf16[16,4,1920]{2,1,0:T(4,128)(2,1)S(1)} fusion(bf16[4,16,1920]{2,0,1:T(4,128)(2,1)S(1)} %copy.15, s32[1024]{0:T(1024)S(1)} %pad_clamp_fusion), kind=kCustom, calls=%fused_computation | custom fusion | bytes 491584 | tf_op jit(solution)/shard_map/jit(_take)/gather | solution.py:39
  8.9 0.2 select_bitcast_fusion
  9.0 17.0 %all_to_all.20 = bf16[4,16,1920]{2,0,1:T(4,128)(2,1)S(1)} all-to-all(bf16[4,16,1920]{2,0,1:T(4,128)(2,1)S(1)} %select_bitcast_fusion), channel_id=1, replica_groups=mesh['grp'=2,'mod'=16] {'mod'}, dimensions={1} | all-to-all | bytes 491520 | tf_op jit(solution)/shard_map/all_to_all | solution.py:40
  26.0 0.0 copy-done
  26.0 8.1 %fusion.11 = f32[16,4,512]{2,0,1:T(8,128)S(1)} fusion(bf16[1,1920,1920]{2,1,0:T(8,128)(2,1)} %param.10, bf16[1,512,1920]{2,1,0:T(8,128)(2,1)S(1)} %copy-done, bf16[4,16,1920]{2,0,1:T(4,128)(2,1)S(1)} %all_to_all.20), kind=kOutput, calls=%fused_computation.8 | convolution fusion | flops 3901685760 | bytes 9715712 | tf_op jit(solution)/shard_map/dot_general | solution.py:42
  34.1 0.1 copy.17
  34.2 10.5 %all_to_all.21 = f32[16,4,512]{2,1,0:T(4,128)S(1)} all-to-all(f32[16,4,512]{2,1,0:T(4,128)S(1)} %copy.17), channel_id=1, replica_groups=mesh['grp'=2,'mod'=16] {'mod'}, dimensions={0} | all-to-all | bytes 262144 | tf_op jit(solution)/shard_map/all_to_all | solution.py:45
  44.7 0.6 %reduce_sum.9 = f32[4,512]{1,0:T(4,128)} reduce(f32[16,4,512]{2,1,0:T(4,128)S(1)} %all_to_all.21, f32[]{:T(128)} %constant.19.clone.1), dimensions={0}, to_apply=%region_1.2 | reduce | flops 30720 | bytes 139268 | tf_op jit(solution)/shard_map/reduce_sum | solution.py:52
  (4 shorter events, 0.0 us)
Async XLA Ops:
  0.0 26.0 %copy-start = (bf16[1,512,1920]{2,1,0:T(8,128)(2,1)S(1)}, bf16[1,512,1920]{2,1,0:T(8,128)(2,1)}, u32[]{:S(2)}) copy-start(bf16[1,512,1920]{2,1,0:T(8,128)(2,1)} %param.11) | copy-start | bytes 5898244

commit v2 on v0

v2 whole, which is shorter than its diff:
```python
import functools

import jax
import jax.numpy as jnp
from jax import lax
from jax.experimental import pallas as pl
from jax.experimental.pallas import tpu as pltpu
from jax.sharding import PartitionSpec as P

OUT_RANK = 40
IN_RANK = 48
SEQ_LEN = 32
LANES = 128
HALF = LANES // 2
HALF_OUT = OUT_RANK // 2
BLOCK_OUT = 5


def form_kernel(examples, modules, owner_ref, lengths_ref, in_ref, out_ref, grads_ref, in_t, out_t, formed):
    rows = examples * modules
    slots = HALF // examples
    base = pl.program_id(0) * slots

    lane = lax.broadcasted_iota(jnp.int32, (modules, LANES), 1)
    module = lax.broadcasted_iota(jnp.int32, (modules, LANES), 0)
    slot = base + (lane % HALF) // examples
    held = lax.fori_loop(
        0, modules, lambda m, own: jnp.where(module == m, owner_ref[m], own), jnp.zeros_like(lane), unroll=modules <= 16
    )
    match = held == slot
    picks = [jnp.where(match & (lane % examples == e), 1.0, 0.0) for e in range(examples)]
    pick = jnp.concatenate(picks, axis=0)
    row_lane = lax.broadcasted_iota(jnp.int32, (rows, LANES), 1)
    low = jnp.where(row_lane < HALF, pick, 0.0).astype(jnp.bfloat16)
    high = jnp.where(row_lane >= HALF, pick, 0.0).astype(jnp.bfloat16)
    pick = pick.astype(jnp.bfloat16)

    over_rows = (((0,), (0,)), ((), ()))
    half_cols = HALF_OUT * SEQ_LEN
    in_t[...] = lax.dot_general(in_ref[...], pick, over_rows, preferred_element_type=jnp.float32)
    turned = lax.dot_general(
        out_ref[:, :half_cols], low, over_rows, preferred_element_type=jnp.float32
    ) + lax.dot_general(out_ref[:, half_cols:], high, over_rows, preferred_element_type=jnp.float32)

    example = lax.broadcasted_iota(jnp.int32, (half_cols, LANES), 1) % examples
    live = jnp.zeros((half_cols, LANES), jnp.int32)
    for e in range(examples):
        live = jnp.where(example == e, lengths_ref[e], live)
    slot_t = lax.broadcasted_iota(jnp.int32, (half_cols, LANES), 0) % SEQ_LEN
    out_t[...] = jnp.where(slot_t < live, turned, 0.0)

    @pl.loop(0, HALF_OUT // BLOCK_OUT)
    def _(block):
        first = block * (BLOCK_OUT * SEQ_LEN)
        sums = [jnp.zeros((IN_RANK, LANES), jnp.float32) for _ in range(BLOCK_OUT)]
        for t in range(SEQ_LEN):
            features = in_t[pl.ds(t, IN_RANK, stride=SEQ_LEN), :]
            for k in range(BLOCK_OUT):
                sums[k] = sums[k] + features * out_t[pl.ds(first + k * SEQ_LEN + t, 1), :]
        start = pl.multiple_of(block * (BLOCK_OUT * IN_RANK), BLOCK_OUT * IN_RANK)
        formed[pl.ds(start, BLOCK_OUT * IN_RANK), :] = jnp.concatenate(sums, axis=0).astype(jnp.bfloat16)

    turned_back = formed[...].T
    grads_ref[...] = jnp.concatenate([turned_back[:HALF], turned_back[HALF:]], axis=1)


def form_grads(inputs_proj, outputs_proj, lengths, owner):
    examples, modules, in_cols = inputs_proj.shape
    out_cols = outputs_proj.shape[2]
    rows = examples * modules
    return pl.pallas_call(
        functools.partial(form_kernel, examples, modules),
        out_shape=jax.ShapeDtypeStruct((rows, OUT_RANK * IN_RANK), jnp.bfloat16),
        grid=(rows // HALF,),
        in_specs=[
            pl.BlockSpec(memory_space=pltpu.SMEM),
            pl.BlockSpec(memory_space=pltpu.SMEM),
            pl.BlockSpec((rows, in_cols), lambda i: (0, 0)),
            pl.BlockSpec((rows, out_cols), lambda i: (0, 0)),
        ],
        out_specs=pl.BlockSpec((HALF, OUT_RANK * IN_RANK), lambda i: (i, 0)),
        scratch_shapes=[
            pltpu.VMEM((in_cols, LANES), jnp.float32),
            pltpu.VMEM((HALF_OUT * SEQ_LEN, LANES), jnp.float32),
            pltpu.VMEM((HALF_OUT * IN_RANK, LANES), jnp.bfloat16),
        ],
        compiler_params=pltpu.CompilerParams(vmem_limit_bytes=24 << 20),
    )(owner, lengths, inputs_proj.reshape(rows, in_cols), outputs_proj.reshape(rows, out_cols))


def score_kernel(grads_ref, fisher_ref, query_ref, scores_ref, total):
    step = pl.program_id(0)

    @pl.when(step == 0)
    def _():
        total[...] = jnp.zeros_like(total)

    solved = jnp.dot(grads_ref[...], fisher_ref[...], preferred_element_type=jnp.float32)
    main = solved.astype(jnp.bfloat16)
    rest = (solved - main.astype(jnp.float32)).astype(jnp.bfloat16)
    rows = main.shape[0]
    both = lax.dot_general(
        jnp.concatenate([main, rest], axis=0),
        query_ref[...],
        (((1,), (1,)), ((), ())),
        preferred_element_type=jnp.float32,
    )
    total[...] += both[:rows] + both[rows:]

    @pl.when(step == pl.num_programs(0) - 1)
    def _():
        scores_ref[...] = total[...].astype(scores_ref.dtype)


def module_scores(grads, fisher, query, columns=384):
    rows, size = grads.shape
    queries = query.shape[0]
    return pl.pallas_call(
        score_kernel,
        out_shape=jax.ShapeDtypeStruct((rows, queries), jnp.bfloat16),
        grid=(size // columns,),
        in_specs=[
            pl.BlockSpec((rows, size), lambda i: (0, 0)),
            pl.BlockSpec((size, columns), lambda i: (0, i)),
            pl.BlockSpec((queries, columns), lambda i: (0, i)),
        ],
        out_specs=pl.BlockSpec((rows, queries), lambda i: (0, 0)),
        scratch_shapes=[pltpu.VMEM((rows, queries), jnp.float32)],
        compiler_params=pltpu.CompilerParams(vmem_limit_bytes=32 << 20),
    )(grads, fisher, query)


def local(inputs_proj, outputs_proj, lengths, owner, fisher_inv, query_grads):
    routed = form_grads(inputs_proj, outputs_proj, lengths, owner)
    received = lax.all_to_all(routed, "mod", split_axis=0, concat_axis=0, tiled=True)
    partial = module_scores(received, fisher_inv[0], query_grads[0])
    spread = lax.all_to_all(partial, "mod", split_axis=0, concat_axis=0, tiled=True)
    groups = spread.reshape(owner.shape[0], inputs_proj.shape[0], spread.shape[1])
    return jnp.sum(groups.astype(jnp.float32), axis=0)


def solution(mesh):
    return jax.shard_map(
        local,
        mesh=mesh,
        in_specs=(
            P(("grp", "mod"), None, None),
            P(("grp", "mod"), None, None),
            P(("grp", "mod")),
            P(),
            P("mod", None, None),
            P("mod", None, None),
        ),
        out_specs=P(("grp", "mod"), None),
        check_vma=False,
    )
```

time: 137 us -> 43.5 us (0.32)
  waiting for transfers between devices: 85.3 us -> 0 us
  between operations: 14.1 us -> 0.04 us
  matrix products: 10.4 us -> 0 us
  blocking collectives: 17 us -> 26.5 us
  Pallas kernels: 0 us -> 8.05 us
    unnamed x2 -> x0, waiting for transfers between devices: 85.3 us -> none
    dot_general x2 -> x0, matrix products: 10.4 us -> none  [the longest x1 8.72 us: local(): lax.dot_general(example_grads, precond, (((1,), (1,)), ((), ())), preferr...]
    all_to_all x1 -> x2, blocking collectives: 17 us -> 26.5 us  [the longest x1 17 us: local(): lax.all_to_all(routed, 'mod', split_axis=0, concat_axis=0, tiled=True)]
    pallas_call x0 -> x2, Pallas kernels: none -> 8.05 us  [the longest x1 4.28 us: module_scores(): pl.pallas_call(score_kernel, out_shape=jax.ShapeDtypeStruct((rows, querie...]
    unnamed x6 -> x12, local copies, waits for them, and re-layouts: 1.92 us -> 7.78 us
    reshape x5 -> x0, local copies, waits for them, and re-layouts: 4.3 us -> none  [the longest x2 3.71 us: masked(): source.reshape(count_rows, count_modules, features, SEQ_LEN)]
  transfers between devices with their start and end apart: 1 -> 0, of which waited for: 1 -> 0; matrix products, arithmetic and copies ran while one was open for 0% -> 0% of each run, Pallas kernels for 0% -> 0%
where the time goes in v2:
time: 43.5 us; the launch traced here: 43.1 us
  blocking collectives  26.5 us (61%)
  Pallas kernels  8.05 us (19%)
  local copies, waits for them, and re-layouts  7.93 us (18%)
  other arithmetic  0.64 us (1%)
    all_to_all x1, blocking collectives, local(): lax.all_to_all(routed, 'mod', split_axis=0, concat_axis=0, tiled=True)  17 us
    all_to_all x1, blocking collectives, local(): lax.all_to_all(partial, 'mod', split_axis=0, concat_axis=0, tiled=True)  9.51 us
    unnamed x12, local copies, waits for them, and re-layouts  7.78 us
    pallas_call x1, Pallas kernels, module_scores(): pl.pallas_call(score_kernel, out_shape=jax.ShapeDtypeStruct((rows, querie...  4.28 us
    pallas_call x1, Pallas kernels, form_grads(): pl.pallas_call(functools.partial(form_kernel, examples, modules), out_sha...  3.77 us

profile of v2, /device:TPU:0, one launch (start us, length us, event | category | flops | bytes accessed | tf_op | source)
XLA Modules:
  0.0 43.1 jit_solution(2653836937965270073)
XLA Ops:
  0.0 0.0 copy-start.2
  0.0 0.9 %copy-done.2 = bf16[4,16,1536]{2,1,0:T(8,128)(2,1)S(1)} copy-done((bf16[4,16,1536]{2,1,0:T(8,128)(2,1)S(1)}, bf16[4,16,1536]{2,1,0:T(8,128)(2,1)}, u32[]{:S(2)}) %copy-start.2) | copy-done | bytes 196632
  0.9 0.0 copy-start.3
  0.9 0.9 %copy-done.3 = bf16[4,16,1280]{2,1,0:T(8,128)(2,1)S(1)} copy-done((bf16[4,16,1280]{2,1,0:T(8,128)(2,1)S(1)}, bf16[4,16,1280]{2,1,0:T(8,128)(2,1)}, u32[]{:S(2)}) %copy-start.3) | copy-done | bytes 163864
  1.8 0.0 copy-start.4
  1.8 0.7 %copy-done.4 = s32[16]{0:T(128)S(1)} copy-done((s32[16]{0:T(128)S(1)}, s32[16]{0:T(128)}, u32[]{:S(2)}) %copy-start.4) | copy-done | bytes 88
  2.5 0.0 copy-start.5
  2.5 0.7 %copy-done.5 = s32[4]{0:T(128)S(1)} copy-done((s32[4]{0:T(128)S(1)}, s32[4]{0:T(128)}, u32[]{:S(2)}) %copy-start.5) | copy-done | bytes 40
  3.2 3.8 %shard_map.64 = bf16[64,1920]{1,0:T(8,128)(2,1)S(1)} custom-call(s32[16]{0:T(128)S(1)} %copy-done.4, s32[4]{0:T(128)S(1)} %copy-done.5, bf16[64,1536]{1,0:T(8,128)(2,1)S(1)} %bitcast.6, bf16[64,1280]{1,0:T(8,128)(2,1)S(1)} %bitcast.7), custom_call_target="tpu_custom_call" | custom-call | tf_op jit(solution)/shard_map/pallas_call | solution.py:71
  6.9 0.1 all_to_all.13
  7.0 17.0 %all_to_all.20 = bf16[16,4,1920]{2,1,0:T(4,128)(2,1)S(1)} all-to-all(bf16[16,4,1920]{2,1,0:T(4,128)(2,1)S(1)} %all_to_all.13), channel_id=1, replica_groups=mesh['grp'=2,'mod'=16] {'mod'}, dimensions={0} | all-to-all | bytes 491520 | tf_op jit(solution)/shard_map/all_to_all | solution.py:135
  24.0 0.1 all_to_all.15.grads_ref
  24.0 0.0 copy-start
  24.0 3.1 %copy-done = bf16[1,1920,1920]{2,1,0:T(8,128)(2,1)S(1)} copy-done((bf16[1,1920,1920]{2,1,0:T(8,128)(2,1)S(1)}, bf16[1,1920,1920]{2,1,0:T(8,128)(2,1)}, u32[]{:S(2)}) %copy-start) | copy-done | bytes 7372824
  27.1 0.0 copy-start.1
  27.1 1.5 %copy-done.1 = bf16[1,512,1920]{2,1,0:T(8,128)(2,1)S(1)} copy-done((bf16[1,512,1920]{2,1,0:T(8,128)(2,1)S(1)}, bf16[1,512,1920]{2,1,0:T(8,128)(2,1)}, u32[]{:S(2)}) %copy-start.1) | copy-done | bytes 1966104
  28.7 4.3 %shard_map.65 = bf16[64,512]{1,0:T(8,128)(2,1)S(1)} custom-call(bf16[64,1920]{1,0:T(8,128)(2,1)S(1)} %all_to_all.15.grads_ref, bf16[1920,1920]{1,0:T(8,128)(2,1)S(1)} %bitcast.4, bf16[512,1920]{1,0:T(8,128)(2,1)S(1)} %bitcast.5), custom_call_target="tpu_custom_call" | custom-call | tf_op jit(solution)/shard_map/pallas_call | solution.py:118
  33.0 9.5 %all_to_all.21 = bf16[16,4,512]{2,1,0:T(4,128)(2,1)S(1)} all-to-all(bf16[16,4,512]{2,1,0:T(4,128)(2,1)S(1)} %all_to_all.16), channel_id=1, replica_groups=mesh['grp'=2,'mod'=16] {'mod'}, dimensions={0} | all-to-all | bytes 131072 | tf_op jit(solution)/shard_map/all_to_all | solution.py:137
  42.5 0.6 %convert_reduce_fusion = f32[4,512]{1,0:T(4,128)} fusion(bf16[16,4,512]{2,1,0:T(4,128)(2,1)S(1)} %all_to_all.21), kind=kLoop, calls=%fused_computation | loop fusion | flops 63488 | bytes 73728 | tf_op jit(solution)/shard_map/reduce_sum | solution.py:139
  (1 shorter events, 0.0 us)
Async XLA Ops:
  0.0 0.9 %copy-start.2 = (bf16[4,16,1536]{2,1,0:T(8,128)(2,1)S(1)}, bf16[4,16,1536]{2,1,0:T(8,128)(2,1)}, u32[]{:S(2)}) copy-start(bf16[4,16,1536]{2,1,0:T(8,128)(2,1)} %param.6) | copy-start | bytes 589828
  0.9 0.9 %copy-start.3 = (bf16[4,16,1280]{2,1,0:T(8,128)(2,1)S(1)}, bf16[4,16,1280]{2,1,0:T(8,128)(2,1)}, u32[]{:S(2)}) copy-start(bf16[4,16,1280]{2,1,0:T(8,128)(2,1)} %param.7) | copy-start | bytes 491524
  1.8 0.7 %copy-start.4 = (s32[16]{0:T(128)S(1)}, s32[16]{0:T(128)}, u32[]{:S(2)}) copy-start(s32[16]{0:T(128)} %owner_ref.1) | copy-start | bytes 196
  2.5 0.7 %copy-start.5 = (s32[4]{0:T(128)S(1)}, s32[4]{0:T(128)}, u32[]{:S(2)}) copy-start(s32[4]{0:T(128)} %lengths_ref.1) | copy-start | bytes 52
  24.0 3.1 %copy-start = (bf16[1,1920,1920]{2,1,0:T(8,128)(2,1)S(1)}, bf16[1,1920,1920]{2,1,0:T(8,128)(2,1)}, u32[]{:S(2)}) copy-start(bf16[1,1920,1920]{2,1,0:T(8,128)(2,1)} %param.10) | copy-start | bytes 22118404
  27.1 1.5 %copy-start.1 = (bf16[1,512,1920]{2,1,0:T(8,128)(2,1)S(1)}, bf16[1,512,1920]{2,1,0:T(8,128)(2,1)}, u32[]{:S(2)}) copy-start(bf16[1,512,1920]{2,1,0:T(8,128)(2,1)} %param.11) | copy-start | bytes 5898244

commit v3 on v2

--- a/solution.py
+++ b/solution.py
@@ -14,10 +14,24 @@
 HALF = LANES // 2
 HALF_OUT = OUT_RANK // 2
 BLOCK_OUT = 5
+LONG = pl.CostEstimate(flops=20_000_000_000, bytes_accessed=30_000_000, transcendentals=0)
 
 
-def form_kernel(examples, modules, owner_ref, lengths_ref, in_ref, out_ref, grads_ref, in_t, out_t, formed):
+def form_kernel(
+    examples, modules, owner_hbm, lengths_hbm, in_hbm, out_hbm, grads_ref,
+    owner_ref, lengths_ref, in_ref, out_ref, in_t, out_t, formed, arrived,
+):
     rows = examples * modules
+    pairs = ((owner_hbm, owner_ref), (lengths_hbm, lengths_ref), (in_hbm, in_ref), (out_hbm, out_ref))
+    copies = [pltpu.make_async_copy(there, here, arrived.at[k]) for k, (there, here) in enumerate(pairs)]
+
+    @pl.when(pl.program_id(0) == 0)
+    def _():
+        for copy in copies:
+            copy.start()
+        for copy in copies:
+            copy.wait()
+
     slots = HALF // examples
     base = pl.program_id(0) * slots
 
@@ -61,82 +75,74 @@
         formed[pl.ds(start, BLOCK_OUT * IN_RANK), :] = jnp.concatenate(sums, axis=0).astype(jnp.bfloat16)
 
     turned_back = formed[...].T
-    grads_ref[...] = jnp.concatenate([turned_back[:HALF], turned_back[HALF:]], axis=1)
+    grads = jnp.concatenate([turned_back[:HALF], turned_back[HALF:]], axis=1)
+    grads_ref[...] = grads.reshape(grads_ref.shape)
 
 
 def form_grads(inputs_proj, outputs_proj, lengths, owner):
     examples, modules, in_cols = inputs_proj.shape
     out_cols = outputs_proj.shape[2]
     rows = examples * modules
+    operands = (owner, lengths, inputs_proj.reshape(rows, in_cols), outputs_proj.reshape(rows, out_cols))
     return pl.pallas_call(
         functools.partial(form_kernel, examples, modules),
-        out_shape=jax.ShapeDtypeStruct((rows, OUT_RANK * IN_RANK), jnp.bfloat16),
+        out_shape=jax.ShapeDtypeStruct((modules, examples, OUT_RANK * IN_RANK), jnp.bfloat16),
         grid=(rows // HALF,),
-        in_specs=[
-            pl.BlockSpec(memory_space=pltpu.SMEM),
-            pl.BlockSpec(memory_space=pltpu.SMEM),
-            pl.BlockSpec((rows, in_cols), lambda i: (0, 0)),
-            pl.BlockSpec((rows, out_cols), lambda i: (0, 0)),
-        ],
-        out_specs=pl.BlockSpec((HALF, OUT_RANK * IN_RANK), lambda i: (i, 0)),
+        in_specs=[pl.BlockSpec(memory_space=pltpu.HBM)] * 4,
+        out_specs=pl.BlockSpec((HALF // examples, examples, OUT_RANK * IN_RANK), lambda i: (i, 0, 0)),
         scratch_shapes=[
+            pltpu.SMEM((modules,), jnp.int32),
+            pltpu.SMEM((examples,), jnp.int32),
+            pltpu.VMEM((rows, in_cols), jnp.bfloat16),
+            pltpu.VMEM((rows, out_cols), jnp.bfloat16),
             pltpu.VMEM((in_cols, LANES), jnp.float32),
             pltpu.VMEM((HALF_OUT * SEQ_LEN, LANES), jnp.float32),
             pltpu.VMEM((HALF_OUT * IN_RANK, LANES), jnp.bfloat16),
+            pltpu.SemaphoreType.DMA((4,)),
         ],
         compiler_params=pltpu.CompilerParams(vmem_limit_bytes=24 << 20),
-    )(owner, lengths, inputs_proj.reshape(rows, in_cols), outputs_proj.reshape(rows, out_cols))
+        cost_estimate=LONG,
+    )(*[pltpu.with_memory_space_constraint(x, pltpu.HBM) for x in operands])
 
 
-def score_kernel(grads_ref, fisher_ref, query_ref, scores_ref, total):
-    step = pl.program_id(0)
-
-    @pl.when(step == 0)
-    def _():
-        total[...] = jnp.zeros_like(total)
-
-    solved = jnp.dot(grads_ref[...], fisher_ref[...], preferred_element_type=jnp.float32)
+def score_kernel(grads_ref, fisher_ref, query_ref, scores_ref):
+    slots, examples, size = grads_ref.shape
+    grads = grads_ref[...].reshape(slots * examples, size)
+    solved = jnp.dot(grads, fisher_ref[0], preferred_element_type=jnp.float32)
     main = solved.astype(jnp.bfloat16)
     rest = (solved - main.astype(jnp.float32)).astype(jnp.bfloat16)
     rows = main.shape[0]
     both = lax.dot_general(
         jnp.concatenate([main, rest], axis=0),
-        query_ref[...],
+        query_ref[0],
         (((1,), (1,)), ((), ())),
         preferred_element_type=jnp.float32,
     )
-    total[...] += both[:rows] + both[rows:]
-
-    @pl.when(step == pl.num_programs(0) - 1)
-    def _():
-        scores_ref[...] = total[...].astype(scores_ref.dtype)
+    scores_ref[...] = (both[:rows] + both[rows:]).astype(scores_ref.dtype).reshape(scores_ref.shape)
 
 
-def module_scores(grads, fisher, query, columns=384):
-    rows, size = grads.shape
-    queries = query.shape[0]
+def module_scores(grads, fisher, query):
+    slots, examples, _ = grads.shape
     return pl.pallas_call(
         score_kernel,
-        out_shape=jax.ShapeDtypeStruct((rows, queries), jnp.bfloat16),
-        grid=(size // columns,),
-        in_specs=[
-            pl.BlockSpec((rows, size), lambda i: (0, 0)),
-            pl.BlockSpec((size, columns), lambda i: (0, i)),
-            pl.BlockSpec((queries, columns), lambda i: (0, i)),
-        ],
-        out_specs=pl.BlockSpec((rows, queries), lambda i: (0, 0)),
-        scratch_shapes=[pltpu.VMEM((rows, queries), jnp.float32)],
-        compiler_params=pltpu.CompilerParams(vmem_limit_bytes=32 << 20),
+        out_shape=jax.ShapeDtypeStruct((slots, examples, query.shape[1]), jnp.bfloat16),
+        in_specs=[pl.BlockSpec(memory_space=pltpu.VMEM)] * 3,
+        out_specs=pl.BlockSpec(memory_space=pltpu.VMEM),
+        compiler_params=pltpu.CompilerParams(vmem_limit_bytes=16 << 20),
+        cost_estimate=pl.CostEstimate(
+            flops=2 * slots * examples * (fisher.size + 2 * query.size),
+            bytes_accessed=2 * (fisher.size + query.size),
+            transcendentals=0,
+        ),
     )(grads, fisher, query)
 
 
 def local(inputs_proj, outputs_proj, lengths, owner, fisher_inv, query_grads):
     routed = form_grads(inputs_proj, outputs_proj, lengths, owner)
     received = lax.all_to_all(routed, "mod", split_axis=0, concat_axis=0, tiled=True)
-    partial = module_scores(received, fisher_inv[0], query_grads[0])
+    partial = module_scores(received, fisher_inv, query_grads)
     spread = lax.all_to_all(partial, "mod", split_axis=0, concat_axis=0, tiled=True)
-    groups = spread.reshape(owner.shape[0], inputs_proj.shape[0], spread.shape[1])
-    return jnp.sum(groups.astype(jnp.float32), axis=0)
+    return jnp.sum(spread.astype(jnp.float32), axis=0)
 
 
 def solution(mesh):

time: 43.5 us -> 33.7 us (0.77)
  local copies, waits for them, and re-layouts: 7.93 us -> 0.01 us
  Pallas kernels: 8.05 us -> 6.39 us
    unnamed x12 -> x4, local copies, waits for them, and re-layouts: 7.78 us -> 0.01 us
    pallas_call x1, Pallas kernels: 4.28 us -> 1.96 us  [module_scores(): pl.pallas_call(score_kernel, out_shape=jax.ShapeDtypeStruct((slots, examp...]
    pallas_call x1, Pallas kernels: 3.77 us -> 4.42 us  [form_grads(): pl.pallas_call(functools.partial(form_kernel, examples, modules), out_sha...]
where the time goes in v3:
time: 33.7 us; the launch traced here: 33.5 us
  blocking collectives  26.5 us (79%)
  Pallas kernels  6.39 us (19%)
  other arithmetic  0.64 us (2%)
    all_to_all x1, blocking collectives, local(): lax.all_to_all(routed, 'mod', split_axis=0, concat_axis=0, tiled=True)  17 us
    all_to_all x1, blocking collectives, local(): lax.all_to_all(partial, 'mod', split_axis=0, concat_axis=0, tiled=True)  9.5 us
    pallas_call x1, Pallas kernels, form_grads(): pl.pallas_call(functools.partial(form_kernel, examples, modules), out_sha...  4.42 us
    pallas_call x1, Pallas kernels, module_scores(): pl.pallas_call(score_kernel, out_shape=jax.ShapeDtypeStruct((slots, examp...  1.96 us

profile of v3, /device:TPU:0, one launch (start us, length us, event | category | flops | bytes accessed | tf_op | source)
XLA Modules:
  0.0 33.5 jit_solution(2757989795264877824)
XLA Ops:
  0.0 0.0 copy-start
  0.0 0.0 copy-start.1
  0.0 4.4 %shard_map.64 = bf16[16,4,1920]{2,1,0:T(4,128)(2,1)S(1)} custom-call(s32[16]{0:T(128)} %owner_hbm.1, s32[4]{0:T(128)} %lengths_hbm.1, bf16[64,1536]{1,0:T(8,128)(2,1)} %bitcast.2, bf16[64,1280]{1,0:T(8,128)(2,1)} %bitcast.3), custom_call_target="tpu_custom_call" | custom-call | flops 20000000000 | bytes 30000000 | tf_op jit(solution)/shard_map/pallas_call | solution.py:87
  4.4 17.0 %all_to_all.10.grads_ref = bf16[16,4,1920]{2,1,0:T(4,128)(2,1)S(1)} all-to-all(bf16[16,4,1920]{2,1,0:T(4,128)(2,1)S(1)} %shard_map.64), channel_id=1, replica_groups=mesh['grp'=2,'mod'=16] {'mod'}, dimensions={0} | all-to-all | bytes 491520 | tf_op jit(solution)/shard_map/all_to_all | solution.py:142
  21.4 0.0 copy-done
  21.4 0.0 copy-done.1
  21.4 2.0 %shard_map.65 = bf16[16,4,512]{2,1,0:T(4,128)(2,1)S(1)} custom-call(bf16[16,4,1920]{2,1,0:T(4,128)(2,1)S(1)} %all_to_all.10.grads_ref, bf16[1,1920,1920]{2,1,0:T(8,128)(2,1)S(1)} %copy-done, bf16[1,512,1920]{2,1,0:T(8,128)(2,1)S(1)} %copy-done.1), custom_call_target="tpu_custom_call" | custom-call | flops 723517440 | bytes 9338880 | tf_op jit(solution)/shard_map/pallas_call | solution.py:126
  23.4 9.5 %all_to_all.11 = bf16[16,4,512]{2,1,0:T(4,128)(2,1)S(1)} all-to-all(bf16[16,4,512]{2,1,0:T(4,128)(2,1)S(1)} %shard_map.65), channel_id=1, replica_groups=mesh['grp'=2,'mod'=16] {'mod'}, dimensions={0} | all-to-all | bytes 131072 | tf_op jit(solution)/shard_map/all_to_all | solution.py:144
  32.9 0.6 %convert_reduce_fusion = f32[4,512]{1,0:T(4,128)} fusion(bf16[16,4,512]{2,1,0:T(4,128)(2,1)S(1)} %all_to_all.11), kind=kLoop, calls=%fused_computation | loop fusion | flops 63488 | bytes 73728 | tf_op jit(solution)/shard_map/reduce_sum | solution.py:145
Async XLA Ops:
  0.0 21.4 %copy-start = (bf16[1,1920,1920]{2,1,0:T(8,128)(2,1)S(1)}, bf16[1,1920,1920]{2,1,0:T(8,128)(2,1)}, u32[]{:S(2)}) copy-start(bf16[1,1920,1920]{2,1,0:T(8,128)(2,1)} %fisher_ref.1) | copy-start | bytes 22118404
  0.0 21.4 %copy-start.1 = (bf16[1,512,1920]{2,1,0:T(8,128)(2,1)S(1)}, bf16[1,512,1920]{2,1,0:T(8,128)(2,1)}, u32[]{:S(2)}) copy-start(bf16[1,512,1920]{2,1,0:T(8,128)(2,1)} %query_ref.1) | copy-start | bytes 5898244

commit v4 on v3

v4 whole, which is shorter than its diff:
```python
import functools

import jax
import jax.numpy as jnp
from jax import lax
from jax.experimental import pallas as pl
from jax.experimental.pallas import tpu as pltpu
from jax.sharding import PartitionSpec as P

OUT_RANK = 40
IN_RANK = 48
SEQ_LEN = 32
LANES = 128
HALF = LANES // 2
HALF_OUT = OUT_RANK // 2
BLOCK_IN = 16
PITCH = SEQ_LEN + 8
LONG = pl.CostEstimate(flops=20_000_000_000, bytes_accessed=30_000_000, transcendentals=0)


def form_kernel(
    examples, owner_hbm, lengths_hbm, in_hbm, out_hbm, grads_ref,
    owner_ref, lengths_ref, in_ref, out_ref, in_t, out_t, formed, arrived,
):
    modules = HALF // examples
    here = pl.ds(pl.program_id(0) * modules, modules)
    pairs = (
        (in_hbm.at[:, here], in_ref),
        (out_hbm.at[:, here], out_ref),
        (lengths_hbm, lengths_ref),
        (owner_hbm, owner_ref),
    )
    copies = [pltpu.make_async_copy(there, mine, arrived.at[k]) for k, (there, mine) in enumerate(pairs)]
    for copy in copies:
        copy.start()
    for copy in copies:
        copy.wait()

    half_cols = HALF_OUT * SEQ_LEN
    inputs = in_ref[...].reshape(HALF, in_ref.shape[2])
    outputs = out_ref[...].reshape(HALF, out_ref.shape[2])
    turned_in = jnp.concatenate([inputs, inputs], axis=0).T.astype(jnp.float32)
    for i in range(IN_RANK):
        in_t[pl.ds(i * PITCH, SEQ_LEN), :] = turned_in[i * SEQ_LEN : (i + 1) * SEQ_LEN]
    turned = jnp.concatenate([outputs[:, :half_cols], outputs[:, half_cols:]], axis=0).T.astype(jnp.float32)

    example = lax.broadcasted_iota(jnp.int32, (half_cols, LANES), 1) % HALF // modules
    live = jnp.zeros((half_cols, LANES), jnp.int32)
    for e in range(examples):
        live = jnp.where(example == e, lengths_ref[e], live)
    slot_t = lax.broadcasted_iota(jnp.int32, (half_cols, LANES), 0) % SEQ_LEN
    out_t[...] = jnp.where(slot_t < live, turned, 0.0)

    @pl.loop(0, IN_RANK // BLOCK_IN)
    def _(block):
        first = block * (BLOCK_IN * PITCH)
        sums = [jnp.zeros((BLOCK_IN, LANES), jnp.float32) for _ in range(HALF_OUT)]
        for t in range(SEQ_LEN):
            features = in_t[pl.ds(first + t, BLOCK_IN, stride=PITCH), :]
            for o in range(HALF_OUT):
                sums[o] = sums[o] + features * out_t[pl.ds(o * SEQ_LEN + t, 1), :]
        for o in range(HALF_OUT):
            start = pl.multiple_of(o * IN_RANK + block * BLOCK_IN, BLOCK_IN)
            formed[pl.ds(start, BLOCK_IN), :] = sums[o].astype(jnp.bfloat16)

    row = lax.broadcasted_iota(jnp.int32, (HALF, HALF), 0)
    lane = lax.broadcasted_iota(jnp.int32, (HALF, HALF), 1)
    pick = jnp.where(lane == row % examples * modules + row // examples, 1.0, 0.0).astype(jnp.bfloat16)
    blank = jnp.zeros_like(pick)
    low = jnp.concatenate([pick, blank], axis=1)
    high = jnp.concatenate([blank, pick], axis=1)

    def take(side, first, last):
        return lax.dot_general(side, formed[first:last], (((1,), (1,)), ((), ())), preferred_element_type=jnp.float32)

    half = HALF_OUT * IN_RANK
    whole = half // LANES * LANES
    parts = [take(low, 0, whole)]
    if whole < half:
        edge = jnp.concatenate([formed[whole:half], formed[: whole + LANES - half]], axis=0)
        upper = lax.broadcasted_iota(jnp.int32, (HALF, LANES), 1) >= half - whole
        over_lanes = (((1,), (1,)), ((), ()))
        parts.append(
            jnp.where(
                upper,
                lax.dot_general(high, edge, over_lanes, preferred_element_type=jnp.float32),
                lax.dot_general(low, edge, over_lanes, preferred_element_type=jnp.float32),
            )
        )
        parts.append(take(high, whole + LANES - half, half))
    else:
        parts.append(take(high, 0, half))
    grads = jnp.concatenate(parts, axis=1).astype(jnp.bfloat16)
    for m in range(modules):
        slot = owner_ref[pl.program_id(0) * modules + m]
        grads_ref[slot] = grads[m * examples : (m + 1) * examples]


def form_grads(inputs_proj, outputs_proj, lengths, owner):
    examples, modules, in_cols = inputs_proj.shape
    out_cols = outputs_proj.shape[2]
    step = HALF // examples
    shape = (modules, examples, OUT_RANK * IN_RANK)
    operands = (owner, lengths, inputs_proj, outputs_proj)
    return pl.pallas_call(
        functools.partial(form_kernel, examples),
        out_shape=jax.ShapeDtypeStruct(shape, jnp.bfloat16),
        grid=(modules // step,),
        in_specs=[pl.BlockSpec(memory_space=pltpu.HBM)] * 4,
        out_specs=pl.BlockSpec(shape, lambda i: (0, 0, 0)),
        scratch_shapes=[
            pltpu.SMEM((modules,), jnp.int32),
            pltpu.SMEM((examples,), jnp.int32),
            pltpu.VMEM((examples, step, in_cols), jnp.bfloat16),
            pltpu.VMEM((examples, step, out_cols), jnp.bfloat16),
            pltpu.VMEM((IN_RANK * PITCH, LANES), jnp.float32),
            pltpu.VMEM((HALF_OUT * SEQ_LEN, LANES), jnp.float32),
            pltpu.VMEM((HALF_OUT * IN_RANK, LANES), jnp.bfloat16),
            pltpu.SemaphoreType.DMA((4,)),
        ],
        compiler_params=pltpu.CompilerParams(vmem_limit_bytes=24 << 20),
        cost_estimate=LONG,
    )(*[pltpu.with_memory_space_constraint(x, pltpu.HBM) for x in operands])


def score_kernel(grads_ref, fisher_ref, query_ref, scores_ref):
    slots, examples, size = grads_ref.shape
    grads = grads_ref[...].reshape(slots * examples, size)
    solved = jnp.dot(grads, fisher_ref[0], preferred_element_type=jnp.float32)
    main = solved.astype(jnp.bfloat16)
    rest = (solved - main.astype(jnp.float32)).astype(jnp.bfloat16)
    rows = main.shape[0]
    both = lax.dot_general(
        jnp.concatenate([main, rest], axis=0),
        query_ref[0],
        (((1,), (1,)), ((), ())),
        preferred_element_type=jnp.float32,
    )
    scores_ref[...] = (both[:rows] + both[rows:]).astype(scores_ref.dtype).reshape(scores_ref.shape)


def module_scores(grads, fisher, query):
    slots, examples, _ = grads.shape
    return pl.pallas_call(
        score_kernel,
        out_shape=jax.ShapeDtypeStruct((slots, examples, query.shape[1]), jnp.bfloat16),
        in_specs=[pl.BlockSpec(memory_space=pltpu.VMEM)] * 3,
        out_specs=pl.BlockSpec(memory_space=pltpu.VMEM),
        compiler_params=pltpu.CompilerParams(vmem_limit_bytes=16 << 20),
        cost_estimate=pl.CostEstimate(
            flops=2 * slots * examples * (fisher.size + 2 * query.size),
            bytes_accessed=2 * (fisher.size + query.size),
            transcendentals=0,
        ),
    )(grads, fisher, query)


def local(inputs_proj, outputs_proj, lengths, owner, fisher_inv, query_grads):
    routed = form_grads(inputs_proj, outputs_proj, lengths, owner)
    received = lax.all_to_all(routed, "mod", split_axis=0, concat_axis=0, tiled=True)
    partial = module_scores(received, fisher_inv, query_grads)
    spread = lax.all_to_all(partial, "mod", split_axis=0, concat_axis=0, tiled=True)
    return jnp.sum(spread.astype(jnp.float32), axis=0)


def solution(mesh):
    return jax.shard_map(
        local,
        mesh=mesh,
        in_specs=(
            P(("grp", "mod"), None, None),
            P(("grp", "mod"), None, None),
            P(("grp", "mod")),
            P(),
            P("mod", None, None),
            P("mod", None, None),
        ),
        out_specs=P(("grp", "mod"), None),
        check_vma=False,
    )
```

time: 33.7 us -> 32.2 us (0.955)
  Pallas kernels: 6.39 us -> 4.87 us
    pallas_call x1, Pallas kernels: 4.42 us -> 2.91 us  [form_grads(): pl.pallas_call(functools.partial(form_kernel, examples), out_shape=jax.Sh...]
where the time goes in v4:
time: 32.2 us; the launch traced here: 32 us
  blocking collectives  26.5 us (82%)
  Pallas kernels  4.87 us (15%)
  other arithmetic  0.64 us (2%)
    all_to_all x1, blocking collectives, local(): lax.all_to_all(routed, 'mod', split_axis=0, concat_axis=0, tiled=True)  17 us
    all_to_all x1, blocking collectives, local(): lax.all_to_all(partial, 'mod', split_axis=0, concat_axis=0, tiled=True)  9.5 us
    pallas_call x1, Pallas kernels, form_grads(): pl.pallas_call(functools.partial(form_kernel, examples), out_shape=jax.Sh...  2.91 us
    pallas_call x1, Pallas kernels, module_scores(): pl.pallas_call(score_kernel, out_shape=jax.ShapeDtypeStruct((slots, examp...  1.96 us

profile of v4, /device:TPU:0, one launch (start us, length us, event | category | flops | bytes accessed | tf_op | source)
XLA Modules:
  0.0 32.0 jit_solution(16971771961085564484)
XLA Ops:
  0.0 0.0 copy-start.1
  0.0 0.0 copy-start
  0.0 2.9 %shard_map.64 = bf16[16,4,1920]{2,1,0:T(4,128)(2,1)S(1)} custom-call(s32[16]{0:T(128)} %owner_hbm.1, s32[4]{0:T(128)} %lengths_hbm.1, bf16[4,16,1536]{2,1,0:T(8,128)(2,1)} %in_hbm.1, bf16[4,16,1280]{2,1,0:T(8,128)(2,1)} %out_hbm.1), custom_call_target="tpu_custom_call" | custom-call | flops 20000000000 | bytes 30000000 | tf_op jit(solution)/shard_map/pallas_call | solution.py:105
  2.9 17.0 %all_to_all.10.grads_ref = bf16[16,4,1920]{2,1,0:T(4,128)(2,1)S(1)} all-to-all(bf16[16,4,1920]{2,1,0:T(4,128)(2,1)S(1)} %shard_map.64), channel_id=1, replica_groups=mesh['grp'=2,'mod'=16] {'mod'}, dimensions={0} | all-to-all | bytes 491520 | tf_op jit(solution)/shard_map/all_to_all | solution.py:160
  19.9 0.0 copy-done.1
  19.9 0.0 copy-done
  19.9 2.0 %shard_map.65 = bf16[16,4,512]{2,1,0:T(4,128)(2,1)S(1)} custom-call(bf16[16,4,1920]{2,1,0:T(4,128)(2,1)S(1)} %all_to_all.10.grads_ref, bf16[1,1920,1920]{2,1,0:T(8,128)(2,1)S(1)} %copy-done, bf16[1,512,1920]{2,1,0:T(8,128)(2,1)S(1)} %copy-done.1), custom_call_target="tpu_custom_call" | custom-call | flops 723517440 | bytes 9338880 | tf_op jit(solution)/shard_map/pallas_call | solution.py:144
  21.9 9.5 %all_to_all.11 = bf16[16,4,512]{2,1,0:T(4,128)(2,1)S(1)} all-to-all(bf16[16,4,512]{2,1,0:T(4,128)(2,1)S(1)} %shard_map.65), channel_id=1, replica_groups=mesh['grp'=2,'mod'=16] {'mod'}, dimensions={0} | all-to-all | bytes 131072 | tf_op jit(solution)/shard_map/all_to_all | solution.py:162
  31.4 0.6 %convert_reduce_fusion = f32[4,512]{1,0:T(4,128)} fusion(bf16[16,4,512]{2,1,0:T(4,128)(2,1)S(1)} %all_to_all.11), kind=kLoop, calls=%fused_computation | loop fusion | flops 63488 | bytes 73728 | tf_op jit(solution)/shard_map/reduce_sum | solution.py:163
Async XLA Ops:
  0.0 19.9 %copy-start.1 = (bf16[1,512,1920]{2,1,0:T(8,128)(2,1)S(1)}, bf16[1,512,1920]{2,1,0:T(8,128)(2,1)}, u32[]{:S(2)}) copy-start(bf16[1,512,1920]{2,1,0:T(8,128)(2,1)} %query_ref.1) | copy-start | bytes 5898244
  0.0 19.9 %copy-start = (bf16[1,1920,1920]{2,1,0:T(8,128)(2,1)S(1)}, bf16[1,1920,1920]{2,1,0:T(8,128)(2,1)}, u32[]{:S(2)}) copy-start(bf16[1,1920,1920]{2,1,0:T(8,128)(2,1)} %fisher_ref.1) | copy-start | bytes 22118404

commit v5 on v4

--- a/solution.py
+++ b/solution.py
@@ -12,9 +12,10 @@
 SEQ_LEN = 32
 LANES = 128
 HALF = LANES // 2
+MXU = 256
 HALF_OUT = OUT_RANK // 2
 BLOCK_IN = 16
-PITCH = SEQ_LEN + 8
+PITCH = SEQ_LEN + 4
 LONG = pl.CostEstimate(flops=20_000_000_000, bytes_accessed=30_000_000, transcendentals=0)
 
 
@@ -123,32 +124,38 @@
     )(*[pltpu.with_memory_space_constraint(x, pltpu.HBM) for x in operands])
 
 
-def score_kernel(grads_ref, fisher_ref, query_ref, scores_ref):
+def score_kernel(grads_ref, fisher_ref, query_ref, scores_ref, grads, turned, solved):
     slots, examples, size = grads_ref.shape
-    grads = grads_ref[...].reshape(slots * examples, size)
-    solved = jnp.dot(grads, fisher_ref[0], preferred_element_type=jnp.float32)
-    main = solved.astype(jnp.bfloat16)
-    rest = (solved - main.astype(jnp.float32)).astype(jnp.bfloat16)
-    rows = main.shape[0]
-    both = lax.dot_general(
-        jnp.concatenate([main, rest], axis=0),
-        query_ref[0],
-        (((1,), (1,)), ((), ())),
-        preferred_element_type=jnp.float32,
+    rows = slots * examples
+    cut = -(-size // 2 // MXU) * MXU
+    grads[...] = grads_ref[...].reshape(rows, size)
+    turned[...] = query_ref[0].T
+    total = jnp.dot(grads[:, :cut], fisher_ref[0, :cut], preferred_element_type=jnp.float32) + jnp.dot(
+        grads[:, cut:], fisher_ref[0, cut:], preferred_element_type=jnp.float32
     )
+    main = total.astype(jnp.bfloat16)
+    rest = (total - main.astype(jnp.float32)).astype(jnp.bfloat16)
+    solved[...] = jnp.concatenate([main, rest], axis=0)
+    both = jnp.dot(solved[...], turned[...], preferred_element_type=jnp.float32)
     scores_ref[...] = (both[:rows] + both[rows:]).astype(scores_ref.dtype).reshape(scores_ref.shape)
 
 
 def module_scores(grads, fisher, query):
-    slots, examples, _ = grads.shape
+    slots, examples, size = grads.shape
+    rows, queries = slots * examples, query.shape[1]
     return pl.pallas_call(
         score_kernel,
-        out_shape=jax.ShapeDtypeStruct((slots, examples, query.shape[1]), jnp.bfloat16),
+        out_shape=jax.ShapeDtypeStruct((slots, examples, queries), jnp.bfloat16),
         in_specs=[pl.BlockSpec(memory_space=pltpu.VMEM)] * 3,
         out_specs=pl.BlockSpec(memory_space=pltpu.VMEM),
-        compiler_params=pltpu.CompilerParams(vmem_limit_bytes=16 << 20),
+        scratch_shapes=[
+            pltpu.VMEM((rows, size), jnp.bfloat16),
+            pltpu.VMEM((size, queries), jnp.bfloat16),
+            pltpu.VMEM((2 * rows, size), jnp.bfloat16),
+        ],
+        compiler_params=pltpu.CompilerParams(vmem_limit_bytes=24 << 20),
         cost_estimate=pl.CostEstimate(
-            flops=2 * slots * examples * (fisher.size + 2 * query.size),
+            flops=2 * rows * (fisher.size + 2 * query.size),
             bytes_accessed=2 * (fisher.size + query.size),
             transcendentals=0,
         ),

time: 32.2 us -> 31.7 us (0.984)
  Pallas kernels: 4.87 us -> 4.33 us
    pallas_call x1, Pallas kernels: 1.96 us -> 1.49 us  [module_scores(): pl.pallas_call(score_kernel, out_shape=jax.ShapeDtypeStruct((slots, examp...]
where the time goes in v5:
time: 31.7 us; the launch traced here: 31.5 us
  blocking collectives  26.5 us (84%)
  Pallas kernels  4.33 us (14%)
  other arithmetic  0.64 us (2%)
    all_to_all x1, blocking collectives, local(): lax.all_to_all(routed, 'mod', split_axis=0, concat_axis=0, tiled=True)  17 us
    all_to_all x1, blocking collectives, local(): lax.all_to_all(partial, 'mod', split_axis=0, concat_axis=0, tiled=True)  9.52 us
    pallas_call x1, Pallas kernels, form_grads(): pl.pallas_call(functools.partial(form_kernel, examples), out_shape=jax.Sh...  2.84 us
    pallas_call x1, Pallas kernels, module_scores(): pl.pallas_call(score_kernel, out_shape=jax.ShapeDtypeStruct((slots, examp...  1.49 us
    reduce_sum x1, other arithmetic, local(): return jnp.sum(spread.astype(jnp.float32), axis=0)  0.64 us

profile of v5, /device:TPU:0, one launch (start us, length us, event | category | flops | bytes accessed | tf_op | source)
XLA Modules:
  0.0 31.5 jit_solution(4130806814300678257)
XLA Ops:
  0.0 0.0 copy-start.1
  0.0 0.0 copy-start
  0.0 2.8 %shard_map.64 = bf16[16,4,1920]{2,1,0:T(4,128)(2,1)S(1)} custom-call(s32[16]{0:T(128)} %owner_hbm.1, s32[4]{0:T(128)} %lengths_hbm.1, bf16[4,16,1536]{2,1,0:T(8,128)(2,1)} %in_hbm.1, bf16[4,16,1280]{2,1,0:T(8,128)(2,1)} %out_hbm.1), custom_call_target="tpu_custom_call" | custom-call | flops 20000000000 | bytes 30000000 | tf_op jit(solution)/shard_map/pallas_call | solution.py:106
  2.9 17.0 %all_to_all.10.grads_ref = bf16[16,4,1920]{2,1,0:T(4,128)(2,1)S(1)} all-to-all(bf16[16,4,1920]{2,1,0:T(4,128)(2,1)S(1)} %shard_map.64), channel_id=1, replica_groups=mesh['grp'=2,'mod'=16] {'mod'}, dimensions={0} | all-to-all | bytes 491520 | tf_op jit(solution)/shard_map/all_to_all | solution.py:167
  19.8 0.0 copy-done.1
  19.8 0.0 copy-done
  19.8 1.5 %shard_map.65 = bf16[16,4,512]{2,1,0:T(4,128)(2,1)S(1)} custom-call(bf16[16,4,1920]{2,1,0:T(4,128)(2,1)S(1)} %all_to_all.10.grads_ref, bf16[1,1920,1920]{2,1,0:T(8,128)(2,1)S(1)} %copy-done, bf16[1,512,1920]{2,1,0:T(8,128)(2,1)S(1)} %copy-done.1), custom_call_target="tpu_custom_call" | custom-call | flops 723517440 | bytes 9338880 | tf_op jit(solution)/shard_map/pallas_call | solution.py:146
  21.3 9.5 %all_to_all.11 = bf16[16,4,512]{2,1,0:T(4,128)(2,1)S(1)} all-to-all(bf16[16,4,512]{2,1,0:T(4,128)(2,1)S(1)} %shard_map.65), channel_id=1, replica_groups=mesh['grp'=2,'mod'=16] {'mod'}, dimensions={0} | all-to-all | bytes 131072 | tf_op jit(solution)/shard_map/all_to_all | solution.py:169
  30.8 0.6 %convert_reduce_fusion = f32[4,512]{1,0:T(4,128)} fusion(bf16[16,4,512]{2,1,0:T(4,128)(2,1)S(1)} %all_to_all.11), kind=kLoop, calls=%fused_computation | loop fusion | flops 63488 | bytes 73728 | tf_op jit(solution)/shard_map/reduce_sum | solution.py:170
Async XLA Ops:
  0.0 19.8 %copy-start.1 = (bf16[1,512,1920]{2,1,0:T(8,128)(2,1)S(1)}, bf16[1,512,1920]{2,1,0:T(8,128)(2,1)}, u32[]{:S(2)}) copy-start(bf16[1,512,1920]{2,1,0:T(8,128)(2,1)} %query_ref.1) | copy-start | bytes 5898244
  0.0 19.8 %copy-start = (bf16[1,1920,1920]{2,1,0:T(8,128)(2,1)S(1)}, bf16[1,1920,1920]{2,1,0:T(8,128)(2,1)}, u32[]{:S(2)}) copy-start(bf16[1,1920,1920]{2,1,0:T(8,128)(2,1)} %fisher_ref.1) | copy-start | bytes 22118404

commit v6 on v5

--- a/solution.py
+++ b/solution.py
@@ -124,7 +124,7 @@
     )(*[pltpu.with_memory_space_constraint(x, pltpu.HBM) for x in operands])
 
 
-def score_kernel(grads_ref, fisher_ref, query_ref, scores_ref, grads, turned, solved):
+def score_kernel(places, grads_ref, fisher_ref, query_ref, scores_ref, grads, turned, solved):
     slots, examples, size = grads_ref.shape
     rows = slots * examples
     cut = -(-size // 2 // MXU) * MXU
@@ -137,14 +137,17 @@
     rest = (total - main.astype(jnp.float32)).astype(jnp.bfloat16)
     solved[...] = jnp.concatenate([main, rest], axis=0)
     both = jnp.dot(solved[...], turned[...], preferred_element_type=jnp.float32)
-    scores_ref[...] = (both[:rows] + both[rows:]).astype(scores_ref.dtype).reshape(scores_ref.shape)
+    scores = (both[:rows] + both[rows:]).astype(scores_ref.dtype)
+    for source, place in enumerate(places):
+        scores_ref[place] = scores[source * examples : (source + 1) * examples]
 
 
-def module_scores(grads, fisher, query):
+def module_scores(grads, fisher, query, order):
     slots, examples, size = grads.shape
     rows, queries = slots * examples, query.shape[1]
+    places = [order.index(source) for source in range(slots)]
     return pl.pallas_call(
-        score_kernel,
+        functools.partial(score_kernel, places),
         out_shape=jax.ShapeDtypeStruct((slots, examples, queries), jnp.bfloat16),
         in_specs=[pl.BlockSpec(memory_space=pltpu.VMEM)] * 3,
         out_specs=pl.BlockSpec(memory_space=pltpu.VMEM),
@@ -165,8 +168,12 @@
 def local(inputs_proj, outputs_proj, lengths, owner, fisher_inv, query_grads):
     routed = form_grads(inputs_proj, outputs_proj, lengths, owner)
     received = lax.all_to_all(routed, "mod", split_axis=0, concat_axis=0, tiled=True)
-    partial = module_scores(received, fisher_inv, query_grads)
-    spread = lax.all_to_all(partial, "mod", split_axis=0, concat_axis=0, tiled=True)
+    count = received.shape[0]
+    far = 2 ** ((count.bit_length() - 1) // 2)
+    near = count // far
+    order = [far_index * near + near_index for near_index in range(near) for far_index in range(far)]
+    partial = module_scores(received, fisher_inv, query_grads, order)
+    spread = lax.all_to_all(partial, "mod", split_axis=0, concat_axis=0, axis_index_groups=[order], tiled=True)
     return jnp.sum(spread.astype(jnp.float32), axis=0)
 
 

time: 31.7 us -> 31.4 us (level)
  no operation moved by 1% of the time
where the time goes in v6:
time: 31.4 us; the launch traced here: 31.2 us
  blocking collectives  26.2 us (83%)
  Pallas kernels  4.33 us (14%)
  other arithmetic  0.64 us (2%)
    all_to_all x1, blocking collectives, local(): lax.all_to_all(routed, 'mod', split_axis=0, concat_axis=0, tiled=True)  17 us
    all_to_all x1, blocking collectives, local(): lax.all_to_all(partial, 'mod', split_axis=0, concat_axis=0, axis_index_gr...  9.25 us
    pallas_call x1, Pallas kernels, form_grads(): pl.pallas_call(functools.partial(form_kernel, examples), out_shape=jax.Sh...  2.84 us
    pallas_call x1, Pallas kernels, module_scores(): pl.pallas_call(functools.partial(score_kernel, places), out_shape=jax.Sha...  1.49 us
    reduce_sum x1, other arithmetic, local(): return jnp.sum(spread.astype(jnp.float32), axis=0)  0.64 us

profile of v6, /device:TPU:0, one launch (start us, length us, event | category | flops | bytes accessed | tf_op | source)
XLA Modules:
  0.0 31.2 jit_solution(3316138652912511151)
XLA Ops:
  0.0 0.0 copy-start.1
  0.0 0.0 copy-start
  0.0 2.8 %shard_map.64 = bf16[16,4,1920]{2,1,0:T(4,128)(2,1)S(1)} custom-call(s32[16]{0:T(128)} %owner_hbm.1, s32[4]{0:T(128)} %lengths_hbm.1, bf16[4,16,1536]{2,1,0:T(8,128)(2,1)} %in_hbm.1, bf16[4,16,1280]{2,1,0:T(8,128)(2,1)} %out_hbm.1), custom_call_target="tpu_custom_call" | custom-call | flops 20000000000 | bytes 30000000 | tf_op jit(solution)/shard_map/pallas_call | solution.py:106
  2.9 17.0 %all_to_all.10.grads_ref = bf16[16,4,1920]{2,1,0:T(4,128)(2,1)S(1)} all-to-all(bf16[16,4,1920]{2,1,0:T(4,128)(2,1)S(1)} %shard_map.64), channel_id=1, replica_groups=mesh['grp'=2,'mod'=16] {'mod'}, dimensions={0} | all-to-all | bytes 491520 | tf_op jit(solution)/shard_map/all_to_all | solution.py:170
  19.8 0.0 copy-done.1
  19.8 0.0 copy-done
  19.8 1.5 %shard_map.65 = bf16[16,4,512]{2,1,0:T(4,128)(2,1)S(1)} custom-call(bf16[16,4,1920]{2,1,0:T(4,128)(2,1)S(1)} %all_to_all.10.grads_ref, bf16[1,1920,1920]{2,1,0:T(8,128)(2,1)S(1)} %copy-done, bf16[1,512,1920]{2,1,0:T(8,128)(2,1)S(1)} %copy-done.1), custom_call_target="tpu_custom_call" | custom-call | flops 723517440 | bytes 9338880 | tf_op jit(solution)/shard_map/pallas_call | solution.py:149
  21.3 9.3 %all_to_all.11 = bf16[16,4,512]{2,1,0:T(4,128)(2,1)S(1)} all-to-all(bf16[16,4,512]{2,1,0:T(4,128)(2,1)S(1)} %shard_map.65), channel_id=1, replica_groups={{0,4,8,12,1,5,9,13,2,6,10,14,3,7,11,15},{16,20,24,28,17,21,25,29,18,22,..., dimensions={0} | all-to-all | bytes 131072 | tf_op jit(solution)/shard_map/all_to_all | solution.py:176
  30.6 0.6 %convert_reduce_fusion = f32[4,512]{1,0:T(4,128)} fusion(bf16[16,4,512]{2,1,0:T(4,128)(2,1)S(1)} %all_to_all.11), kind=kLoop, calls=%fused_computation | loop fusion | flops 63488 | bytes 73728 | tf_op jit(solution)/shard_map/reduce_sum | solution.py:177
Async XLA Ops:
  0.0 19.8 %copy-start.1 = (bf16[1,512,1920]{2,1,0:T(8,128)(2,1)S(1)}, bf16[1,512,1920]{2,1,0:T(8,128)(2,1)}, u32[]{:S(2)}) copy-start(bf16[1,512,1920]{2,1,0:T(8,128)(2,1)} %query_ref.1) | copy-start | bytes 5898244
  0.0 19.8 %copy-start = (bf16[1,1920,1920]{2,1,0:T(8,128)(2,1)S(1)}, bf16[1,1920,1920]{2,1,0:T(8,128)(2,1)}, u32[]{:S(2)}) copy-start(bf16[1,1920,1920]{2,1,0:T(8,128)(2,1)} %fisher_ref.1) | copy-start | bytes 22118404

commit v7 on v5

--- a/solution.py
+++ b/solution.py
@@ -17,6 +17,22 @@
 BLOCK_IN = 16
 PITCH = SEQ_LEN + 4
 LONG = pl.CostEstimate(flops=20_000_000_000, bytes_accessed=30_000_000, transcendentals=0)
+
+
+def first_listed(count):
+    return 3 * count // 4 - 1
+
+
+def listed(count):
+    order = list(range(count))[::-1]
+    first = order.index(first_listed(count))
+    order[0], order[first] = order[first], order[0]
+    return order
+
+
+def place_of(slot, count):
+    first, last = first_listed(count), count - 1
+    return jnp.where(slot == first, 0, jnp.where(slot == last, last - first, last - slot))
 
 
 def form_kernel(
@@ -94,7 +110,7 @@
     grads = jnp.concatenate(parts, axis=1).astype(jnp.bfloat16)
     for m in range(modules):
         slot = owner_ref[pl.program_id(0) * modules + m]
-        grads_ref[slot] = grads[m * examples : (m + 1) * examples]
+        grads_ref[place_of(slot, grads_ref.shape[0])] = grads[m * examples : (m + 1) * examples]
 
 
 def form_grads(inputs_proj, outputs_proj, lengths, owner):
@@ -163,10 +179,11 @@
 
 
 def local(inputs_proj, outputs_proj, lengths, owner, fisher_inv, query_grads):
+    groups = [listed(owner.shape[0])]
     routed = form_grads(inputs_proj, outputs_proj, lengths, owner)
-    received = lax.all_to_all(routed, "mod", split_axis=0, concat_axis=0, tiled=True)
+    received = lax.all_to_all(routed, "mod", split_axis=0, concat_axis=0, axis_index_groups=groups, tiled=True)
     partial = module_scores(received, fisher_inv, query_grads)
-    spread = lax.all_to_all(partial, "mod", split_axis=0, concat_axis=0, tiled=True)
+    spread = lax.all_to_all(partial, "mod", split_axis=0, concat_axis=0, axis_index_groups=groups, tiled=True)
     return jnp.sum(spread.astype(jnp.float32), axis=0)
 
 

time: 31.7 us -> 27.3 us (0.86)
  blocking collectives: 26.5 us -> 22.1 us
    all_to_all x2, blocking collectives: 26.5 us -> 22.1 us  [the longest x1 13.4 us: local(): lax.all_to_all(routed, 'mod', split_axis=0, concat_axis=0, axis_index_gro...]
where the time goes in v7:
time: 27.3 us; the launch traced here: 27.1 us
  blocking collectives  22.1 us (81%)
  Pallas kernels  4.33 us (16%)
  other arithmetic  0.64 us (2%)
    all_to_all x1, blocking collectives, local(): lax.all_to_all(routed, 'mod', split_axis=0, concat_axis=0, axis_index_gro...  13.4 us
    all_to_all x1, blocking collectives, local(): lax.all_to_all(partial, 'mod', split_axis=0, concat_axis=0, axis_index_gr...  8.67 us
    pallas_call x1, Pallas kernels, form_grads(): pl.pallas_call(functools.partial(form_kernel, examples), out_shape=jax.Sh...  2.84 us
    pallas_call x1, Pallas kernels, module_scores(): pl.pallas_call(score_kernel, out_shape=jax.ShapeDtypeStruct((slots, examp...  1.49 us
    reduce_sum x1, other arithmetic, local(): return jnp.sum(spread.astype(jnp.float32), axis=0)  0.64 us

profile of v7, /device:TPU:0, one launch (start us, length us, event | category | flops | bytes accessed | tf_op | source)
XLA Modules:
  0.0 27.1 jit_solution(16250821093251155404)
XLA Ops:
  0.0 0.0 copy-start.1
  0.0 0.0 copy-start
  0.0 2.8 %shard_map.64 = bf16[16,4,1920]{2,1,0:T(4,128)(2,1)S(1)} custom-call(s32[16]{0:T(128)} %owner_hbm.1, s32[4]{0:T(128)} %lengths_hbm.1, bf16[4,16,1536]{2,1,0:T(8,128)(2,1)} %in_hbm.1, bf16[4,16,1280]{2,1,0:T(8,128)(2,1)} %out_hbm.1), custom_call_target="tpu_custom_call" | custom-call | flops 20000000000 | bytes 30000000 | tf_op jit(solution)/shard_map/pallas_call | solution.py:122
  2.9 13.4 %all_to_all.10.grads_ref = bf16[16,4,1920]{2,1,0:T(4,128)(2,1)S(1)} all-to-all(bf16[16,4,1920]{2,1,0:T(4,128)(2,1)S(1)} %shard_map.64), channel_id=1, replica_groups={{11,14,13,12,15,10,9,8,7,6,5,4,3,2,1,0},{27,30,29,28,31,26,25,24,23,22,..., dimensions={0} | all-to-all | bytes 491520 | tf_op jit(solution)/shard_map/all_to_all | solution.py:184
  16.3 0.0 copy-done.1
  16.3 0.0 copy-done
  16.3 1.5 %shard_map.65 = bf16[16,4,512]{2,1,0:T(4,128)(2,1)S(1)} custom-call(bf16[16,4,1920]{2,1,0:T(4,128)(2,1)S(1)} %all_to_all.10.grads_ref, bf16[1,1920,1920]{2,1,0:T(8,128)(2,1)S(1)} %copy-done, bf16[1,512,1920]{2,1,0:T(8,128)(2,1)S(1)} %copy-done.1), custom_call_target="tpu_custom_call" | custom-call | flops 723517440 | bytes 9338880 | tf_op jit(solution)/shard_map/pallas_call | solution.py:162
  17.8 8.7 %all_to_all.11 = bf16[16,4,512]{2,1,0:T(4,128)(2,1)S(1)} all-to-all(bf16[16,4,512]{2,1,0:T(4,128)(2,1)S(1)} %shard_map.65), channel_id=1, replica_groups={{11,14,13,12,15,10,9,8,7,6,5,4,3,2,1,0},{27,30,29,28,31,26,25,24,23,22,..., dimensions={0} | all-to-all | bytes 131072 | tf_op jit(solution)/shard_map/all_to_all | solution.py:186
  26.4 0.6 %convert_reduce_fusion = f32[4,512]{1,0:T(4,128)} fusion(bf16[16,4,512]{2,1,0:T(4,128)(2,1)S(1)} %all_to_all.11), kind=kLoop, calls=%fused_computation | loop fusion | flops 63488 | bytes 73728 | tf_op jit(solution)/shard_map/reduce_sum | solution.py:187
Async XLA Ops:
  0.0 16.3 %copy-start.1 = (bf16[1,512,1920]{2,1,0:T(8,128)(2,1)S(1)}, bf16[1,512,1920]{2,1,0:T(8,128)(2,1)}, u32[]{:S(2)}) copy-start(bf16[1,512,1920]{2,1,0:T(8,128)(2,1)} %query_ref.1) | copy-start | bytes 5898244
  0.0 16.3 %copy-start = (bf16[1,1920,1920]{2,1,0:T(8,128)(2,1)S(1)}, bf16[1,1920,1920]{2,1,0:T(8,128)(2,1)}, u32[]{:S(2)}) copy-start(bf16[1,1920,1920]{2,1,0:T(8,128)(2,1)} %fisher_ref.1) | copy-start | bytes 22118404

commit v8 on v7

--- a/solution.py
+++ b/solution.py
@@ -28,6 +28,18 @@
     first = order.index(first_listed(count))
     order[0], order[first] = order[first], order[0]
     return order
+
+
+def listed_by_distance(count):
+    first = first_listed(count)
+    near = count // 2 ** ((count.bit_length() - 1) // 2)
+
+    def distance(device):
+        apart = abs(device // near - first // near) + abs(device % near // 2 - first % near // 2)
+        return (apart, device % 2 != first % 2)
+
+    others = sorted((device for device in range(count) if device != first), key=distance, reverse=True)
+    return [first, *others]
 
 
 def place_of(slot, count):
@@ -140,7 +152,7 @@
     )(*[pltpu.with_memory_space_constraint(x, pltpu.HBM) for x in operands])
 
 
-def score_kernel(grads_ref, fisher_ref, query_ref, scores_ref, grads, turned, solved):
+def score_kernel(places, grads_ref, fisher_ref, query_ref, scores_ref, grads, turned, solved):
     slots, examples, size = grads_ref.shape
     rows = slots * examples
     cut = -(-size // 2 // MXU) * MXU
@@ -153,14 +165,16 @@
     rest = (total - main.astype(jnp.float32)).astype(jnp.bfloat16)
     solved[...] = jnp.concatenate([main, rest], axis=0)
     both = jnp.dot(solved[...], turned[...], preferred_element_type=jnp.float32)
-    scores_ref[...] = (both[:rows] + both[rows:]).astype(scores_ref.dtype).reshape(scores_ref.shape)
-
-
-def module_scores(grads, fisher, query):
+    scores = (both[:rows] + both[rows:]).astype(scores_ref.dtype)
+    for block, place in enumerate(places):
+        scores_ref[place] = scores[block * examples : (block + 1) * examples]
+
+
+def module_scores(grads, fisher, query, places):
     slots, examples, size = grads.shape
     rows, queries = slots * examples, query.shape[1]
     return pl.pallas_call(
-        score_kernel,
+        functools.partial(score_kernel, places),
         out_shape=jax.ShapeDtypeStruct((slots, examples, queries), jnp.bfloat16),
         in_specs=[pl.BlockSpec(memory_space=pltpu.VMEM)] * 3,
         out_specs=pl.BlockSpec(memory_space=pltpu.VMEM),
@@ -179,11 +193,12 @@
 
 
 def local(inputs_proj, outputs_proj, lengths, owner, fisher_inv, query_grads):
-    groups = [listed(owner.shape[0])]
+    count = owner.shape[0]
+    out, back = listed(count), listed_by_distance(count)
     routed = form_grads(inputs_proj, outputs_proj, lengths, owner)
-    received = lax.all_to_all(routed, "mod", split_axis=0, concat_axis=0, axis_index_groups=groups, tiled=True)
-    partial = module_scores(received, fisher_inv, query_grads)
-    spread = lax.all_to_all(partial, "mod", split_axis=0, concat_axis=0, axis_index_groups=groups, tiled=True)
+    received = lax.all_to_all(routed, "mod", split_axis=0, concat_axis=0, axis_index_groups=[out], tiled=True)
+    partial = module_scores(received, fisher_inv, query_grads, [back.index(device) for device in out])
+    spread = lax.all_to_all(partial, "mod", split_axis=0, concat_axis=0, axis_index_groups=[back], tiled=True)
     return jnp.sum(spread.astype(jnp.float32), axis=0)
 
 

time: 27.3 us -> 27.2 us (level)
  no operation moved by 1% of the time
where the time goes in v8:
time: 27.2 us; the launch traced here: 27 us
  blocking collectives  22 us (81%)
  Pallas kernels  4.33 us (16%)
  other arithmetic  0.64 us (2%)
    all_to_all x1, blocking collectives, local(): lax.all_to_all(routed, 'mod', split_axis=0, concat_axis=0, axis_index_gro...  13.4 us
    all_to_all x1, blocking collectives, local(): lax.all_to_all(partial, 'mod', split_axis=0, concat_axis=0, axis_index_gr...  8.59 us
    pallas_call x1, Pallas kernels, form_grads(): pl.pallas_call(functools.partial(form_kernel, examples), out_shape=jax.Sh...  2.84 us
    pallas_call x1, Pallas kernels, module_scores(): pl.pallas_call(functools.partial(score_kernel, places), out_shape=jax.Sha...  1.49 us
    reduce_sum x1, other arithmetic, local(): return jnp.sum(spread.astype(jnp.float32), axis=0)  0.64 us

profile of v8, /device:TPU:0, one launch (start us, length us, event | category | flops | bytes accessed | tf_op | source)
XLA Modules:
  0.0 27.0 jit_solution(9800065829451148057)
XLA Ops:
  0.0 0.0 copy-start.1
  0.0 0.0 copy-start
  0.0 2.8 %shard_map.64 = bf16[16,4,1920]{2,1,0:T(4,128)(2,1)S(1)} custom-call(s32[16]{0:T(128)} %owner_hbm.1, s32[4]{0:T(128)} %lengths_hbm.1, bf16[4,16,1536]{2,1,0:T(8,128)(2,1)} %in_hbm.1, bf16[4,16,1280]{2,1,0:T(8,128)(2,1)} %out_hbm.1), custom_call_target="tpu_custom_call" | custom-call | flops 20000000000 | bytes 30000000 | tf_op jit(solution)/shard_map/pallas_call | solution.py:134
  2.9 13.4 %all_to_all.10.grads_ref = bf16[16,4,1920]{2,1,0:T(4,128)(2,1)S(1)} all-to-all(bf16[16,4,1920]{2,1,0:T(4,128)(2,1)S(1)} %shard_map.64), channel_id=1, replica_groups={{11,14,13,12,15,10,9,8,7,6,5,4,3,2,1,0},{27,30,29,28,31,26,25,24,23,22,..., dimensions={0} | all-to-all | bytes 491520 | tf_op jit(solution)/shard_map/all_to_all | solution.py:199
  16.3 0.0 copy-done.1
  16.3 0.0 copy-done
  16.3 1.5 %shard_map.65 = bf16[16,4,512]{2,1,0:T(4,128)(2,1)S(1)} custom-call(bf16[16,4,1920]{2,1,0:T(4,128)(2,1)S(1)} %all_to_all.10.grads_ref, bf16[1,1920,1920]{2,1,0:T(8,128)(2,1)S(1)} %copy-done, bf16[1,512,1920]{2,1,0:T(8,128)(2,1)S(1)} %copy-done.1), custom_call_target="tpu_custom_call" | custom-call | flops 723517440 | bytes 9338880 | tf_op jit(solution)/shard_map/pallas_call | solution.py:176
  17.8 8.6 %all_to_all.11 = bf16[16,4,512]{2,1,0:T(4,128)(2,1)S(1)} all-to-all(bf16[16,4,512]{2,1,0:T(4,128)(2,1)S(1)} %shard_map.65), channel_id=1, replica_groups={{11,0,1,2,4,12,3,5,13,6,8,14,7,9,15,10},{27,16,17,18,20,28,19,21,29,22,..., dimensions={0} | all-to-all | bytes 131072 | tf_op jit(solution)/shard_map/all_to_all | solution.py:201
  26.3 0.6 %convert_reduce_fusion = f32[4,512]{1,0:T(4,128)} fusion(bf16[16,4,512]{2,1,0:T(4,128)(2,1)S(1)} %all_to_all.11), kind=kLoop, calls=%fused_computation | loop fusion | flops 63488 | bytes 73728 | tf_op jit(solution)/shard_map/reduce_sum | solution.py:202
Async XLA Ops:
  0.0 16.3 %copy-start.1 = (bf16[1,512,1920]{2,1,0:T(8,128)(2,1)S(1)}, bf16[1,512,1920]{2,1,0:T(8,128)(2,1)}, u32[]{:S(2)}) copy-start(bf16[1,512,1920]{2,1,0:T(8,128)(2,1)} %query_ref.1) | copy-start | bytes 5898244
  0.0 16.3 %copy-start = (bf16[1,1920,1920]{2,1,0:T(8,128)(2,1)S(1)}, bf16[1,1920,1920]{2,1,0:T(8,128)(2,1)}, u32[]{:S(2)}) copy-start(bf16[1,1920,1920]{2,1,0:T(8,128)(2,1)} %fisher_ref.1) | copy-start | bytes 22118404

commit v9 on v8

--- a/solution.py
+++ b/solution.py
@@ -24,10 +24,8 @@
 
 
 def listed(count):
-    order = list(range(count))[::-1]
-    first = order.index(first_listed(count))
-    order[0], order[first] = order[first], order[0]
-    return order
+    first = first_listed(count)
+    return [(first - place) % count for place in range(count)]
 
 
 def listed_by_distance(count):
@@ -43,8 +41,8 @@
 
 
 def place_of(slot, count):
-    first, last = first_listed(count), count - 1
-    return jnp.where(slot == first, 0, jnp.where(slot == last, last - first, last - slot))
+    behind = first_listed(count) - slot
+    return jnp.where(behind < 0, behind + count, behind)
 
 
 def form_kernel(

time: 27.2 us -> 27.2 us (level)
  no operation moved by 1% of the time
where the time goes in v9:
time: 27.2 us; the launch traced here: 27 us
  blocking collectives  22 us (81%)
  Pallas kernels  4.33 us (16%)
  other arithmetic  0.64 us (2%)
    all_to_all x1, blocking collectives, local(): lax.all_to_all(routed, 'mod', split_axis=0, concat_axis=0, axis_index_gro...  13.4 us
    all_to_all x1, blocking collectives, local(): lax.all_to_all(partial, 'mod', split_axis=0, concat_axis=0, axis_index_gr...  8.58 us
    pallas_call x1, Pallas kernels, form_grads(): pl.pallas_call(functools.partial(form_kernel, examples), out_shape=jax.Sh...  2.84 us
    pallas_call x1, Pallas kernels, module_scores(): pl.pallas_call(functools.partial(score_kernel, places), out_shape=jax.Sha...  1.49 us
    reduce_sum x1, other arithmetic, local(): return jnp.sum(spread.astype(jnp.float32), axis=0)  0.64 us

profile of v9, /device:TPU:0, one launch (start us, length us, event | category | flops | bytes accessed | tf_op | source)
XLA Modules:
  0.0 27.0 jit_solution(471538858182801831)
XLA Ops:
  0.0 0.0 copy-start.1
  0.0 0.0 copy-start
  0.0 2.8 %shard_map.64 = bf16[16,4,1920]{2,1,0:T(4,128)(2,1)S(1)} custom-call(s32[16]{0:T(128)} %owner_hbm.1, s32[4]{0:T(128)} %lengths_hbm.1, bf16[4,16,1536]{2,1,0:T(8,128)(2,1)} %in_hbm.1, bf16[4,16,1280]{2,1,0:T(8,128)(2,1)} %out_hbm.1), custom_call_target="tpu_custom_call" | custom-call | flops 20000000000 | bytes 30000000 | tf_op jit(solution)/shard_map/pallas_call | solution.py:132
  2.9 13.4 %all_to_all.10.grads_ref = bf16[16,4,1920]{2,1,0:T(4,128)(2,1)S(1)} all-to-all(bf16[16,4,1920]{2,1,0:T(4,128)(2,1)S(1)} %shard_map.64), channel_id=1, replica_groups={{11,10,9,8,7,6,5,4,3,2,1,0,15,14,13,12},{27,26,25,24,23,22,21,20,19,18,..., dimensions={0} | all-to-all | bytes 491520 | tf_op jit(solution)/shard_map/all_to_all | solution.py:197
  16.3 0.0 copy-done.1
  16.3 0.0 copy-done
  16.3 1.5 %shard_map.65 = bf16[16,4,512]{2,1,0:T(4,128)(2,1)S(1)} custom-call(bf16[16,4,1920]{2,1,0:T(4,128)(2,1)S(1)} %all_to_all.10.grads_ref, bf16[1,1920,1920]{2,1,0:T(8,128)(2,1)S(1)} %copy-done, bf16[1,512,1920]{2,1,0:T(8,128)(2,1)S(1)} %copy-done.1), custom_call_target="tpu_custom_call" | custom-call | flops 723517440 | bytes 9338880 | tf_op jit(solution)/shard_map/pallas_call | solution.py:174
  17.8 8.6 %all_to_all.11 = bf16[16,4,512]{2,1,0:T(4,128)(2,1)S(1)} all-to-all(bf16[16,4,512]{2,1,0:T(4,128)(2,1)S(1)} %shard_map.65), channel_id=1, replica_groups={{11,0,1,2,4,12,3,5,13,6,8,14,7,9,15,10},{27,16,17,18,20,28,19,21,29,22,..., dimensions={0} | all-to-all | bytes 131072 | tf_op jit(solution)/shard_map/all_to_all | solution.py:199
  26.3 0.6 %convert_reduce_fusion = f32[4,512]{1,0:T(4,128)} fusion(bf16[16,4,512]{2,1,0:T(4,128)(2,1)S(1)} %all_to_all.11), kind=kLoop, calls=%fused_computation | loop fusion | flops 63488 | bytes 73728 | tf_op jit(solution)/shard_map/reduce_sum | solution.py:200
Async XLA Ops:
  0.0 16.3 %copy-start.1 = (bf16[1,512,1920]{2,1,0:T(8,128)(2,1)S(1)}, bf16[1,512,1920]{2,1,0:T(8,128)(2,1)}, u32[]{:S(2)}) copy-start(bf16[1,512,1920]{2,1,0:T(8,128)(2,1)} %query_ref.1) | copy-start | bytes 5898244
  0.0 16.3 %copy-start = (bf16[1,1920,1920]{2,1,0:T(8,128)(2,1)S(1)}, bf16[1,1920,1920]{2,1,0:T(8,128)(2,1)}, u32[]{:S(2)}) copy-start(bf16[1,1920,1920]{2,1,0:T(8,128)(2,1)} %fisher_ref.1) | copy-start | bytes 22118404
